TPU v7x, 32 devices: a whole 2x2x4 slice. The times are simulated.
32 devices in a mesh: member: 8 (over y, x, core), band: 4 (over z).
Axes of the slice: x: 2, y: 2, z: 4, core: 2. Of those that a mesh axis runs over, the one named last changes fastest.
Arguments:
- controls: float32 [16, 16, 256, 512], P('member', None, 'band'), may hold values from -6 to 6
- members: float32 [16, 16, 256, 512], P('member', None, 'band'), may hold values from -6 to 6
- loc_lon: float32 [512, 512], replicated, may hold values from -0.25 to 0.25
- loc_lat: float32 [256, 256], replicated, may hold values from -0.375 to 0.375
- balance: float32 [5, 1024, 2048], P(None, 'band', 'member'), may hold values from -1 to 1
- innovation: float32 [16, 1024, 2048], P(None, 'band', 'member'), may hold values from -6 to 6
- obs_weight: float32 [16, 1024, 2048], P(None, 'band', 'member'), may hold values from 0.2 to 5
Outputs:
- gradient: float32 [16, 16, 256, 512], P('member', None, 'band')
All inputs are finite; a program needn't handle non-finite values.
Results may differ from a plain program's by a relative error of at most 0.00012.
Values sent between devices are 32-bit elements; how exact they have to be, the bound alone decides.
No kernel may reach another device: no remote copies, remote signals or barrier semaphores. Data moves between devices by JAX's collectives and lax.ppermute only.
A program may use at most 128 MiB of HBM per device.

v0:
```python
import math
import jax
import jax.numpy as jnp
from jax import lax
from jax.sharding import PartitionSpec as P

phase_fraction = (0.625, 0.875, 0.125, 0.375)
phase_start = (0, 0, 1, 1)


def with_halo(value, sides, width, wrap):
    for axis, dim in sides:
        size, length = (lax.axis_size(axis), value.shape[dim])
        up = [(i, (i + 1) % size) for i in range(size if wrap else size - 1)]
        down = [(j, i) for i, j in up]
        last = lax.slice_in_dim(value, length - width, length, axis=dim)
        leading = lax.slice_in_dim(value, 0, width, axis=dim)
        before = lax.ppermute(last, axis, up)
        after = lax.ppermute(leading, axis, down)
        value = jnp.concatenate([before, value, after], axis=dim)
    return value


def passed_along(value, axis, by):
    length = lax.axis_size(axis)
    return lax.ppermute(value, axis, [(i, (i + by) % length) for i in range(length)])


def from_behind(value, axis, steps):
    count = lax.axis_size(axis)
    leading, last = (max(0, -steps), min(count, count - steps))
    return lax.ppermute(value, axis, [(source, source + steps) for source in range(leading, last)])


def cubic_weights(fraction):
    return (
        (-(fraction**3) + 2 * fraction**2 - fraction) / 2,
        (3 * fraction**3 - 5 * fraction**2 + 2) / 2,
        (-3 * fraction**3 + 4 * fraction**2 + fraction) / 2,
        (fraction**3 - fraction**2) / 2,
    )


def refine(padded, dim_index):
    length = padded.shape[dim_index] - 4
    phase_rows = []
    for phase_index in range(4):
        weights = cubic_weights(phase_fraction[phase_index])
        summed = jnp.zeros_like(lax.slice_in_dim(padded, 0, length, axis=dim_index))
        for tap_index in range(4):
            first = phase_start[phase_index] + tap_index
            summed = summed + weights[tap_index] * lax.slice_in_dim(
                padded, first, first + length, axis=dim_index
            )
        phase_rows.append(summed)
    stacked = jnp.stack(phase_rows, axis=dim_index + 1)
    new_shape = list(padded.shape)
    new_shape[dim_index] = 4 * length
    return stacked.reshape(new_shape)


def refine_both(padded):
    return refine(refine(padded, 1), 2)


def body(controls, members, loc_lon, loc_lat, balance, innovation, obs_weight):
    highest = lax.Precision.HIGHEST
    member_scale = 1.0 / math.sqrt(controls.shape[0] * lax.axis_size("member") - 1)
    full_lon = loc_lon.shape[0]
    stripe_width = full_lon // lax.axis_size("member")
    level_ctrl, level_members = (
        lax.all_to_all(controls, "band", split_axis=1, concat_axis=2, tiled=True),
        lax.all_to_all(members, "band", split_axis=1, concat_axis=2, tiled=True),
    )
    rowwise = jnp.einsum("klyx,ux->klyu", level_ctrl, loc_lon, precision=highest)
    fields = jnp.einsum("vy,klyx->klvx", loc_lat, rowwise, precision=highest)
    partial_value = jnp.sum(level_members * fields, axis=0) * member_scale
    summed = lax.psum(partial_value, "member")
    summed = lax.all_to_all(summed, "band", split_axis=1, concat_axis=0, tiled=True)
    wrapped = jnp.concatenate([summed[:, :, -2:], summed, summed[:, :, :2]], axis=2)
    extended = lax.dynamic_slice_in_dim(
        wrapped, lax.axis_index("member") * stripe_width, stripe_width + 4, 2
    )
    padded = with_halo(extended, (("band", 1),), 2, False)
    fine_field = refine_both(padded)
    grown_field = with_halo(fine_field, (("member", 2),), 1, True)
    grown_field = with_halo(grown_field, (("band", 1),), 1, False)
    balanced = (
        balance[0] * fine_field
        + balance[1] * grown_field[:, 1:-1, 2:]
        + balance[2] * grown_field[:, 1:-1, :-2]
        + balance[3] * grown_field[:, 2:, 1:-1]
        + balance[4] * grown_field[:, :-2, 1:-1]
    )
    weighted_misfit = obs_weight * (balanced - innovation)
    pieces = balance[1:, None] * weighted_misfit[None]
    spread = with_halo(pieces, (("member", 3),), 1, True)
    spread = with_halo(spread, (("band", 2),), 1, False)
    fine_grad = (
        balance[0] * weighted_misfit
        + spread[0][:, 1:-1, :-2]
        + spread[1][:, 1:-1, 2:]
        + spread[2][:, :-2, 1:-1]
        + spread[3][:, 2:, 1:-1]
    )
    unused, pullback = jax.vjp(refine_both, padded)
    coarse_ext = pullback(fine_grad)[0]
    west_rim = passed_along(coarse_ext[:, :, :2], "member", -1)
    east_rim = passed_along(coarse_ext[:, :, -2:], "member", 1)
    core_sum = coarse_ext[:, :, 2:-2]
    core_sum = core_sum.at[:, :, -2:].add(west_rim)
    core_sum = core_sum.at[:, :, :2].add(east_rim)
    south_rim = from_behind(core_sum[:, :2], "band", -1)
    north_rim = from_behind(core_sum[:, -2:], "band", 1)
    coarse_grad = core_sum[:, 2:-2]
    coarse_grad = coarse_grad.at[:, -2:].add(south_rim)
    coarse_grad = coarse_grad.at[:, :2].add(north_rim)
    level_grad = lax.all_to_all(coarse_grad, "band", split_axis=0, concat_axis=1, tiled=True)
    weighted = (
        level_members
        * lax.all_gather(level_grad, "member", axis=2, tiled=True)[None]
        * member_scale
    )
    adjoint = jnp.einsum("klyu,ux->klyx", weighted, loc_lon, precision=highest)
    adjoint = jnp.einsum("vy,klvx->klyx", loc_lat, adjoint, precision=highest)
    adjoint = lax.all_to_all(adjoint, "band", split_axis=2, concat_axis=1, tiled=True)
    return controls + adjoint


def solution(mesh):
    return jax.shard_map(
        body,
        mesh=mesh,
        in_specs=(
            P("member", None, "band", None),
            P("member", None, "band", None),
            P(),
            P(),
            P(None, "band", "member"),
            P(None, "band", "member"),
            P(None, "band", "member"),
        ),
        out_specs=P("member", None, "band", None),
        check_vma=False,
    )
```

profile of v0, /device:TPU:0, one launch (start us, length us, event | category | flops | bytes accessed | tf_op | source)
XLA Modules:
  0.0 769.8 jit_solution(10708017313778358526)
XLA Ops:
  11.5 6.3 all-to-all-start
  22.8 88.5 %all-to-all-done = f32[2,16,64,512]{3,2,0,1:T(8,128)} async-done(((f32[2,16,64,512]{3,2,0,1:T(8,128)}), f32[2,16,64,512]{3,2,0,1:T(8,128)}, u32[]{:S(2)}, u32[]{:S(2)}) %all-to-all-start) | async-done | bytes 4194336 | tf_op jit(solution)/shard_map/all_to_all | solution.py:73
  126.4 82.4 %all-to-all-done.1 = f32[2,16,64,512]{3,2,0,1:T(8,128)} async-done(((f32[2,16,64,512]{3,2,0,1:T(8,128)}), f32[2,16,64,512]{3,2,0,1:T(8,128)}, u32[]{:S(2)}, u32[]{:S(2)}) %all-to-all-start.1) | async-done | bytes 4194336 | tf_op jit(solution)/shard_map/all_to_all | solution.py:72
  211.6 7.2 fusion.20
  224.4 61.1 %all-reduce.34.cloned.1.call-done = f32[4,256,512]{1,2,0:T(8,128)} async-done(((f32[4,256,512]{1,2,0:T(8,128)}), f32[4,256,512]{1,2,0:T(8,128)}) %all-reduce.34.cloned.1.call-update) | async-done | bytes 2097168 | tf_op jit(solution)/shard_map/psum | solution.py:78
  293.3 46.9 %all-to-all-done.2 = f32[4,256,512]{2,0,1:T(4,128)S(1)} async-done(((f32[4,256,512]{2,0,1:T(4,128)}), f32[4,256,512]{2,0,1:T(4,128)S(1)}, u32[]{:S(2)}, u32[]{:S(2)}) %all-to-all-start.2) | async-done | bytes 2097184 | tf_op jit(solution)/shard_map/all_to_all | solution.py:79
  357.1 8.6 %copy.114 = f32[16,256,64,4]{1,0,3,2:T(8,128)} copy(f32[16,256,64,4]{2,0,1,3:T(8,128)} %pad_maximum_fusion.2) | data formatting | bytes 8388608 | tf_op jit(solution)/shard_map/stack | solution.py:56
  406.6 20.2 %fusion.3 = f32[16,256,256]{1,0,2:T(8,128)} fusion(f32[16,256,256]{1,0,2:T(8,128)} %copy.124, f32[16,256,256]{1,0,2:T(8,128)} %copy.123, f32[16,1,258]{1,0,2:T(8,128)} %copy.122, f32[16,256,1]{1,0,2:T(8,128)S(1)} %collective-permute-done.2, f32[16,256,256]{1,0,2:T(8,128)} %bitcast.240, f32[16,256,1]{1,0,2:T(8,128)S(1)} %collective-permute-done.3, ...), kind=kLoop, calls=%fused_computation.17 | loop fusion | flops 19922944 | bytes 18153728 | tf_op jit(solution)/shard_map/mul | solution.py:95
  426.8 10.8 %broadcast_multiply_fusion = f32[4,16,256,256]{2,1,3,0:T(8,128)} fusion(f32[16,256,256]{1,0,2:T(8,128)} %fusion.3, f32[4,256,256]{1,2,0:T(8,128)} %copy.125), kind=kLoop, calls=%fused_computation.3 | loop fusion | flops 4194304 | bytes 22020096 | tf_op jit(solution)/shard_map/mul | solution.py:96
  443.8 6.8 pad_maximum_fusion.1
  450.6 7.3 fusion.39
  457.9 6.5 copy.126
  467.5 6.5 copy.127
  475.5 6.4 copy.128
  481.9 6.3 copy.129
  488.2 25.8 %pad_maximum_fusion = f32[4,16,258,258]{2,1,3,0:T(8,128)} fusion(f32[4,16,1,258]{2,1,3,0:T(8,128)} %copy.129, f32[4,16,256,1]{2,1,3,0:T(8,128)S(1)} %collective-permute-done.7, f32[4,16,256,256]{2,1,3,0:T(8,128)} %broadcast_multiply_fusion, f32[4,16,256,1]{2,1,3,0:T(8,128)S(1)} %collective-permute-done.6, f32[4,16,1,258]{2,1,3,0:T(8,128)} %copy.128), kind=kLoop, calls=%fused_computation | loop fusion | flops 17040384 | bytes 34080768 | tf_op jit(solution)/shard_map/concatenate | solution.py:20
  514.1 17.6 %slice_bitcast_fusion.3 = (f32[16,258,258]{1,0,2:T(8,128)}, f32[16,258,258]{1,0,2:T(8,128)}, f32[16,258,258]{1,0,2:T(8,128)}, f32[16,258,258]{1,0,2:T(8,128)}) fusion(f32[4,16,258,258]{2,1,3,0:T(8,128)} %pad_maximum_fusion), kind=kLoop, calls=%fused_computation.7 | loop fusion | bytes 34080768 | tf_op jit(solution)/shard_map/squeeze | solution.py:101
  531.7 9.4 %slice_add_fusion = f32[16,256,256]{1,0,2:T(8,128)S(1)} fusion(f32[16,258,258]{1,0,2:T(8,128)} %get-tuple-element.56, f32[16,258,258]{1,0,2:T(8,128)} %get-tuple-element.57, f32[16,258,258]{1,0,2:T(8,128)} %get-tuple-element.58, f32[16,258,258]{1,0,2:T(8,128)} %get-tuple-element.55, f32[16,256,256]{1,0,2:T(8,128)S(1)} %copy-done.1, f32[256,256]{0,1:T(8,128)S(1)} %copy.102), kind=kLoop, calls=%fused_computation.9 | loop fusion | flops 5242880 | bytes 25427968 | tf_op jit(solution)/shard_map/add | solution.py:100
  558.5 15.6 %scatter-add.14 = f32[16,68,64]{2,0,1:T(8,128)S(1)} dynamic-update-slice(f32[16,68,64]{2,0,1:T(8,128)S(1)} %slice.339, f32[16,68,2]{2,0,1:T(8,128)S(1)} %slice_add_fusion.4, s32[]{:T(128)} %constant.132.clone.1, s32[]{:T(128)} %constant.132.clone.1, s32[]{:T(128)} %constant.145.clone.1) | dynamic-update-slice | bytes 17412 | tf_op jit(solution)/shard_map/scatter-add | solution.py:111
  574.8 7.0 scatter-add.15
  590.4 13.3 %all_to_all.90 = f32[4,1,16384]{2,1,0:T(1,128)S(1)} all-to-all(f32[4,1,16384]{2,1,0:T(1,128)S(1)} %reshape.202), channel_id=1, replica_groups=mesh['member'=8,'band'=4] {'band'}, dimensions={0} | all-to-all | bytes 524288 | tf_op jit(solution)/shard_map/all_to_all | solution.py:118
  607.2 27.2 %all-gather.2.cloned.1.call-done = f32[4,256,512]{1,2,0:T(8,128)} async-done(((f32[4,256,64]{1,2,0:T(8,128)}), f32[4,256,512]{1,2,0:T(8,128)}) %all-gather.2.cloned.1.call-update) | async-done | bytes 2097168 | tf_op jit(solution)/shard_map/all_gather | solution.py:121
  636.3 9.8 %fusion.11 = f32[2,4,256,512]{2,3,1,0:T(8,128)S(1)} fusion(f32[2,4,256,512]{3,2,1,0:T(8,128)} %bitcast.242, f32[4,256,512]{2,1,0:T(8,128)S(1)} %copy.154, f32[512,512]{1,0:T(8,128)S(1)} %copy-done), kind=kOutput, calls=%fused_computation.33 | convolution fusion | flops 6444548096 | bytes 11534336 | tf_op jit(solution)/shard_map/klyu,ux->klyx/dot_general | solution.py:124
  656.5 98.4 %all_to_all.91 = f32[2,4,256,512]{3,1,0,2:T(4,128)S(1)} all-to-all(f32[2,4,256,512]{3,1,0,2:T(4,128)} %copy.156), channel_id=1, replica_groups=mesh['member'=8,'band'=4] {'band'}, dimensions={2} | all-to-all | bytes 8388608 | tf_op jit(solution)/shard_map/all_to_all | solution.py:126
  (117 shorter events, 159.6 us)
Async XLA Ops:
  6.5 205.0 %copy-start = (f32[512,512]{1,0:T(8,128)S(1)}, f32[512,512]{1,0:T(8,128)}, u32[]{:S(2)}) copy-start(f32[512,512]{1,0:T(8,128)} %param.17) | copy-start | bytes 3145732
  11.5 99.8 %all-to-all-start = ((f32[2,16,64,512]{3,2,0,1:T(8,128)}), f32[2,16,64,512]{3,2,0,1:T(8,128)}, u32[]{:S(2)}, u32[]{:S(2)}) async-start(f32[2,16,64,512]{3,2,0,1:T(8,128)} %copy.99), calls=%async_computation | async-start | bytes 8388608 | tf_op jit(solution)/shard_map/all_to_all | solution.py:73
  111.3 97.5 %all-to-all-start.1 = ((f32[2,16,64,512]{3,2,0,1:T(8,128)}), f32[2,16,64,512]{3,2,0,1:T(8,128)}, u32[]{:S(2)}, u32[]{:S(2)}) async-start(f32[2,16,64,512]{3,2,0,1:T(8,128)} %copy.103), calls=%async_computation.1 | async-start | bytes 8388608 | tf_op jit(solution)/shard_map/all_to_all | solution.py:72
  116.2 169.3 %all-reduce.34.cloned.1.call-start = ((), (), s32[]{:S(2)}) async-start(), calls=%async_computation.5 | async-start | bytes 4194304 | tf_op jit(solution)/shard_map/psum | solution.py:78
  211.5 7.2 copy-start.3
  211.5 7.2 copy-start.4
  288.6 51.6 %all-to-all-start.2 = ((f32[4,256,512]{2,0,1:T(4,128)}), f32[4,256,512]{2,0,1:T(4,128)S(1)}, u32[]{:S(2)}, u32[]{:S(2)}) async-start(f32[4,256,512]{2,0,1:T(4,128)} %copy.108), calls=%async_computation.2 | async-start | bytes 4194304 | tf_op jit(solution)/shard_map/all_to_all | solution.py:79
  293.1 341.3 %all-gather.2.cloned.1.call-start = ((), (), s32[]{:S(2)}) async-start(), calls=%async_computation.6 | async-start | bytes 2359296 | tf_op jit(solution)/shard_map/all_gather | solution.py:121
  341.8 2.7 collective-permute-start
  343.1 5.6 collective-permute-start.1
  366.5 1.4 collective-permute-start.2
  366.5 4.1 collective-permute-start.3
  377.9 24.7 %collective-permute-start.4 = (f32[16,1,258]{2,0,1:T(8,128)S(1)}, f32[16,1,258]{2,0,1:T(8,128)S(1)}, u32[]{:S(2)}, u32[]{:S(2)}) collective-permute-start(f32[16,1,258]{2,0,1:T(8,128)S(1)} %copy.118), channel_id=1, source_target_pairs={{1,0},{2,1},{3,2},{5,4},{6,5},{7,6},{9,8},{10,9},{11,10},{13,12},{... | collective-permute-start | bytes 49544 | tf_op jit(solution)/shard_map/ppermute | solution.py:19
  380.3 23.7 %collective-permute-start.5 = (f32[16,1,258]{2,0,1:T(8,128)S(1)}, f32[16,1,258]{2,0,1:T(8,128)S(1)}, u32[]{:S(2)}, u32[]{:S(2)}) collective-permute-start(f32[16,1,258]{2,0,1:T(8,128)S(1)} %copy.121), channel_id=1, source_target_pairs={{0,1},{1,2},{2,3},{4,5},{5,6},{6,7},{8,9},{9,10},{10,11},{12,13},{... | collective-permute-start | bytes 49544 | tf_op jit(solution)/shard_map/ppermute | solution.py:18
  438.4 5.3 collective-permute-start.6
  438.5 5.3 collective-permute-start.7
  464.4 11.1 %collective-permute-start.8 = (f32[4,16,1,258]{3,1,2,0:T(8,128)S(1)}, f32[4,16,1,258]{3,1,2,0:T(8,128)S(1)}, u32[]{:S(2)}, u32[]{:S(2)}) collective-permute-start(f32[4,16,1,258]{3,1,2,0:T(8,128)S(1)} %copy.126), channel_id=1, source_target_pairs={{0,1},{1,2},{2,3},{4,5},{5,6},{6,7},{8,9},{9,10},{10,11},{12,13},{... | collective-permute-start | bytes 198152 | tf_op jit(solution)/shard_map/ppermute | solution.py:18
  474.0 7.9 %collective-permute-start.9 = (f32[4,16,1,258]{3,1,2,0:T(8,128)S(1)}, f32[4,16,1,258]{3,1,2,0:T(8,128)S(1)}, u32[]{:S(2)}, u32[]{:S(2)}) collective-permute-start(f32[4,16,1,258]{3,1,2,0:T(8,128)S(1)} %copy.127), channel_id=1, source_target_pairs={{1,0},{2,1},{3,2},{5,4},{6,5},{7,6},{9,8},{10,9},{11,10},{13,12},{... | collective-permute-start | bytes 198152 | tf_op jit(solution)/shard_map/ppermute | solution.py:19
  514.1 17.6 %copy-start.1 = (f32[16,256,256]{1,0,2:T(8,128)S(1)}, f32[16,256,256]{1,0,2:T(8,128)}, u32[]{:S(2)}) copy-start(f32[16,256,256]{1,0,2:T(8,128)} %fusion.3) | copy-start | bytes 12582916
  554.8 3.1 collective-permute-start.10
  557.0 17.4 %collective-permute-start.11 = (f32[16,68,2]{1,0,2:T(8,128)S(1)}, f32[16,68,2]{1,0,2:T(8,128)S(1)}, u32[]{:S(2)}, u32[]{:S(2)}) collective-permute-start(f32[16,68,2]{1,0,2:T(8,128)S(1)} %copy.149), channel_id=1, source_target_pairs={{0,4},{4,8},{8,12},{12,16},{16,20},{20,24},{24,28},{28,0},{1,5},{5... | collective-permute-start | bytes 26120 | tf_op jit(solution)/shard_map/ppermute | solution.py:26
  581.9 6.5 collective-permute-start.12
  583.2 6.6 collective-permute-start.13
  636.3 9.8 %copy-start.5 = (f32[256,256]{1,0:T(8,128)S(1)}, f32[256,256]{1,0:T(8,128)}, u32[]{:S(2)}) copy-start(f32[256,256]{1,0:T(8,128)} %param.18) | copy-start | bytes 786436
  (2 other events, 7.7 us)
Sparse Core Ops, SparseCore 0:
  224.5 60.9 all-reduce.33
  607.3 27.0 all-gather.1
where the time goes:
time: 780 us; the launch traced here: 770 us
  waiting for transfers between devices  319 us (41%)
  local copies, waits for them, and re-layouts  158 us (20%)
  blocking collectives  112 us (14%)
  other arithmetic  100 us (13%)
  starting transfers between devices  40.8 us (5%)
  matrix products  25.9 us (3%)
  between operations  14.3 us (2%)
    all_to_all x1, blocking collectives, body(): lax.all_to_all(adjoint, 'band', split_axis=2, concat_axis=1, tiled=True)  98.4 us
    all_to_all x1, waiting for transfers between devices, body(): lax.all_to_all(members, 'band', split_axis=1, concat_axis=2, tiled=True)  88.5 us
    all_to_all x1, waiting for transfers between devices, body(): lax.all_to_all(controls, 'band', split_axis=1, concat_axis=2, tiled=True)  82.4 us
    psum x1, waiting for transfers between devices, body(): summed = lax.psum(partial_value, 'member')  61.1 us
    all_to_all x1, waiting for transfers between devices, body(): lax.all_to_all(summed, 'band', split_axis=1, concat_axis=0, tiled=True)  46.9 us
    concatenate x3, other arithmetic, with_halo(): value = jnp.concatenate([before, value, after], axis=dim)  35.3 us
    all_gather x1, waiting for transfers between devices, body(): lax.all_gather(level_grad, 'member', axis=2, tiled=True)[None]  27.2 us
    unnamed x18, local copies, waits for them, and re-layouts  23.1 us
  transfers between devices with their start and end apart: 19, of which 12 were waited for; matrix products, arithmetic and copies ran while one was open for 8% of the time, Pallas kernels for 0%

commit v1 on v0

--- a/solution.py
+++ b/solution.py
@@ -123,7 +123,10 @@
     )
     adjoint = jnp.einsum("klyu,ux->klyx", weighted, loc_lon, precision=highest)
     adjoint = jnp.einsum("vy,klvx->klyx", loc_lat, adjoint, precision=highest)
-    adjoint = lax.all_to_all(adjoint, "band", split_axis=2, concat_axis=1, tiled=True)
+    peers = lax.axis_size("band")
+    blocks = jnp.stack(jnp.split(adjoint, peers, axis=2), axis=0)
+    blocks = lax.all_to_all(blocks, "band", split_axis=0, concat_axis=0)
+    adjoint = jnp.concatenate(blocks, axis=1)
     return controls + adjoint
 
 

time: 780 us -> 772 us (0.990)
  transfers between devices with their start and end apart: 19 -> 19, of which waited for: 12 -> 12; matrix products, arithmetic and copies ran while one was open for 8% -> 9% of each run, Pallas kernels for 0% -> 0%
where the time goes in v1:
time: 772 us; the launch traced here: 762 us
  waiting for transfers between devices  319 us (41%)
  local copies, waits for them, and re-layouts  151 us (20%)
  blocking collectives  111 us (14%)
  other arithmetic  101 us (13%)
  starting transfers between devices  40.8 us (5%)
  matrix products  25 us (3%)
  between operations  14.3 us (2%)
    all_to_all x1, blocking collectives, body(): blocks = lax.all_to_all(blocks, 'band', split_axis=0, concat_axis=0)  97.9 us
    all_to_all x1, waiting for transfers between devices, body(): lax.all_to_all(members, 'band', split_axis=1, concat_axis=2, tiled=True)  88.5 us
    all_to_all x1, waiting for transfers between devices, body(): lax.all_to_all(controls, 'band', split_axis=1, concat_axis=2, tiled=True)  82.4 us
    psum x1, waiting for transfers between devices, body(): summed = lax.psum(partial_value, 'member')  61.1 us
    all_to_all x1, waiting for transfers between devices, body(): lax.all_to_all(summed, 'band', split_axis=1, concat_axis=0, tiled=True)  46.9 us
    concatenate x3, other arithmetic, with_halo(): value = jnp.concatenate([before, value, after], axis=dim)  35.3 us
    all_gather x1, waiting for transfers between devices, body(): lax.all_gather(level_grad, 'member', axis=2, tiled=True)[None]  27.2 us
    unnamed x18, local copies, waits for them, and re-layouts  23.1 us
  transfers between devices with their start and end apart: 19, of which 12 were waited for; matrix products, arithmetic and copies ran while one was open for 9% of the time, Pallas kernels for 0%

profile of v1, /device:TPU:0, one launch (start us, length us, event | category | flops | bytes accessed | tf_op | source)
XLA Modules:
  0.0 761.9 jit_solution(12941199593423471205)
XLA Ops:
  11.5 6.3 all-to-all-start
  22.8 88.5 %all-to-all-done = f32[2,16,64,512]{3,2,0,1:T(8,128)} async-done(((f32[2,16,64,512]{3,2,0,1:T(8,128)}), f32[2,16,64,512]{3,2,0,1:T(8,128)}, u32[]{:S(2)}, u32[]{:S(2)}) %all-to-all-start) | async-done | bytes 4194336 | tf_op jit(solution)/shard_map/all_to_all | solution.py:73
  126.4 82.4 %all-to-all-done.1 = f32[2,16,64,512]{3,2,0,1:T(8,128)} async-done(((f32[2,16,64,512]{3,2,0,1:T(8,128)}), f32[2,16,64,512]{3,2,0,1:T(8,128)}, u32[]{:S(2)}, u32[]{:S(2)}) %all-to-all-start.1) | async-done | bytes 4194336 | tf_op jit(solution)/shard_map/all_to_all | solution.py:72
  211.6 7.2 fusion.20
  224.4 61.1 %all-reduce.34.cloned.1.call-done = f32[4,256,512]{1,2,0:T(8,128)} async-done(((f32[4,256,512]{1,2,0:T(8,128)}), f32[4,256,512]{1,2,0:T(8,128)}) %all-reduce.34.cloned.1.call-update) | async-done | bytes 2097168 | tf_op jit(solution)/shard_map/psum | solution.py:78
  293.3 46.9 %all-to-all-done.2 = f32[4,256,512]{2,0,1:T(4,128)S(1)} async-done(((f32[4,256,512]{2,0,1:T(4,128)}), f32[4,256,512]{2,0,1:T(4,128)S(1)}, u32[]{:S(2)}, u32[]{:S(2)}) %all-to-all-start.2) | async-done | bytes 2097184 | tf_op jit(solution)/shard_map/all_to_all | solution.py:79
  357.1 8.5 %copy.114 = f32[16,256,64,4]{1,0,3,2:T(8,128)} copy(f32[16,256,64,4]{2,0,1,3:T(8,128)} %pad_maximum_fusion.2) | data formatting | bytes 8388608 | tf_op jit(solution)/shard_map/stack | solution.py:56
  406.5 20.0 %fusion.3 = f32[16,256,256]{1,0,2:T(8,128)} fusion(f32[16,256,256]{1,0,2:T(8,128)} %copy.124, f32[16,256,256]{1,0,2:T(8,128)} %copy.123, f32[16,1,258]{1,0,2:T(8,128)} %copy.122, f32[16,256,1]{1,0,2:T(8,128)S(1)} %collective-permute-done.2, f32[16,256,256]{1,0,2:T(8,128)} %bitcast.247, f32[16,256,1]{1,0,2:T(8,128)S(1)} %collective-permute-done.3, ...), kind=kLoop, calls=%fused_computation.17 | loop fusion | flops 19922944 | bytes 18153728 | tf_op jit(solution)/shard_map/mul | solution.py:95
  426.5 10.8 %broadcast_multiply_fusion = f32[4,16,256,256]{2,1,3,0:T(8,128)} fusion(f32[16,256,256]{1,0,2:T(8,128)} %fusion.3, f32[4,256,256]{1,2,0:T(8,128)} %copy.125), kind=kLoop, calls=%fused_computation.3 | loop fusion | flops 4194304 | bytes 22020096 | tf_op jit(solution)/shard_map/mul | solution.py:96
  443.5 6.8 pad_maximum_fusion.1
  450.3 7.3 fusion.39
  457.6 6.5 copy.126
  467.2 6.5 copy.127
  475.2 6.4 copy.128
  481.6 6.3 copy.129
  487.9 25.8 %pad_maximum_fusion = f32[4,16,258,258]{2,1,3,0:T(8,128)} fusion(f32[4,16,1,258]{2,1,3,0:T(8,128)} %copy.129, f32[4,16,256,1]{2,1,3,0:T(8,128)S(1)} %collective-permute-done.7, f32[4,16,256,256]{2,1,3,0:T(8,128)} %broadcast_multiply_fusion, f32[4,16,256,1]{2,1,3,0:T(8,128)S(1)} %collective-permute-done.6, f32[4,16,1,258]{2,1,3,0:T(8,128)} %copy.128), kind=kLoop, calls=%fused_computation | loop fusion | flops 17040384 | bytes 34080768 | tf_op jit(solution)/shard_map/concatenate | solution.py:20
  513.8 17.6 %slice_bitcast_fusion.3 = (f32[16,258,258]{1,0,2:T(8,128)}, f32[16,258,258]{1,0,2:T(8,128)}, f32[16,258,258]{1,0,2:T(8,128)}, f32[16,258,258]{1,0,2:T(8,128)}) fusion(f32[4,16,258,258]{2,1,3,0:T(8,128)} %pad_maximum_fusion), kind=kLoop, calls=%fused_computation.7 | loop fusion | bytes 34080768 | tf_op jit(solution)/shard_map/squeeze | solution.py:101
  531.4 9.4 %slice_add_fusion = f32[16,256,256]{1,0,2:T(8,128)S(1)} fusion(f32[16,258,258]{1,0,2:T(8,128)} %get-tuple-element.56, f32[16,258,258]{1,0,2:T(8,128)} %get-tuple-element.57, f32[16,258,258]{1,0,2:T(8,128)} %get-tuple-element.58, f32[16,258,258]{1,0,2:T(8,128)} %get-tuple-element.55, f32[16,256,256]{1,0,2:T(8,128)S(1)} %copy-done.1, f32[256,256]{0,1:T(8,128)S(1)} %copy.102), kind=kLoop, calls=%fused_computation.9 | loop fusion | flops 5242880 | bytes 25427968 | tf_op jit(solution)/shard_map/add | solution.py:100
  558.5 15.6 %scatter-add.14 = f32[16,68,64]{2,0,1:T(8,128)S(1)} dynamic-update-slice(f32[16,68,64]{2,0,1:T(8,128)S(1)} %slice.339, f32[16,68,2]{2,0,1:T(8,128)S(1)} %slice_add_fusion.4, s32[]{:T(128)} %constant.132.clone.1, s32[]{:T(128)} %constant.132.clone.1, s32[]{:T(128)} %constant.145.clone.1) | dynamic-update-slice | bytes 17412 | tf_op jit(solution)/shard_map/scatter-add | solution.py:111
  574.8 7.0 scatter-add.15
  590.3 13.1 %all_to_all.77 = f32[4,1,16384]{2,1,0:T(1,128)S(1)} all-to-all(f32[4,1,16384]{2,1,0:T(1,128)S(1)} %reshape.211), channel_id=1, replica_groups=mesh['member'=8,'band'=4] {'band'}, dimensions={0} | all-to-all | bytes 524288 | tf_op jit(solution)/shard_map/all_to_all | solution.py:118
  606.8 27.2 %all-gather.2.cloned.1.call-done = f32[4,256,512]{1,2,0:T(8,128)} async-done(((f32[4,256,64]{1,2,0:T(8,128)}), f32[4,256,512]{1,2,0:T(8,128)}) %all-gather.2.cloned.1.call-update) | async-done | bytes 2097168 | tf_op jit(solution)/shard_map/all_gather | solution.py:121
  636.2 9.2 %fusion.11 = f32[2,4,256,512]{3,2,1,0:T(8,128)S(1)} fusion(f32[2,4,256,512]{3,2,1,0:T(8,128)} %bitcast.249, f32[4,256,512]{2,1,0:T(8,128)S(1)} %copy.154, f32[512,512]{1,0:T(8,128)S(1)} %copy-done), kind=kOutput, calls=%fused_computation.34 | convolution fusion | flops 6444548096 | bytes 11534336 | tf_op jit(solution)/shard_map/klyu,ux->klyx/dot_general | solution.py:124
  651.5 97.9 %all_to_all.78 = f32[4,2,4,64,512]{4,3,2,1,0:T(8,128)S(1)} all-to-all(f32[4,2,4,64,512]{4,3,2,1,0:T(8,128)S(1)} %pad_maximum_fusion.12), channel_id=1, replica_groups=mesh['member'=8,'band'=4] {'band'}, dimensions={0} | all-to-all | bytes 8388608 | tf_op jit(solution)/shard_map/all_to_all | solution.py:128
  (117 shorter events, 153.0 us)
Async XLA Ops:
  6.5 205.0 %copy-start = (f32[512,512]{1,0:T(8,128)S(1)}, f32[512,512]{1,0:T(8,128)}, u32[]{:S(2)}) copy-start(f32[512,512]{1,0:T(8,128)} %param.17) | copy-start | bytes 3145732
  11.5 99.8 %all-to-all-start = ((f32[2,16,64,512]{3,2,0,1:T(8,128)}), f32[2,16,64,512]{3,2,0,1:T(8,128)}, u32[]{:S(2)}, u32[]{:S(2)}) async-start(f32[2,16,64,512]{3,2,0,1:T(8,128)} %copy.99), calls=%async_computation | async-start | bytes 8388608 | tf_op jit(solution)/shard_map/all_to_all | solution.py:73
  111.3 97.5 %all-to-all-start.1 = ((f32[2,16,64,512]{3,2,0,1:T(8,128)}), f32[2,16,64,512]{3,2,0,1:T(8,128)}, u32[]{:S(2)}, u32[]{:S(2)}) async-start(f32[2,16,64,512]{3,2,0,1:T(8,128)} %copy.103), calls=%async_computation.1 | async-start | bytes 8388608 | tf_op jit(solution)/shard_map/all_to_all | solution.py:72
  116.2 169.4 %all-reduce.34.cloned.1.call-start = ((), (), s32[]{:S(2)}) async-start(), calls=%async_computation.5 | async-start | bytes 4194304 | tf_op jit(solution)/shard_map/psum | solution.py:78
  211.6 7.2 copy-start.3
  211.6 7.2 copy-start.4
  288.6 51.6 %all-to-all-start.2 = ((f32[4,256,512]{2,0,1:T(4,128)}), f32[4,256,512]{2,0,1:T(4,128)S(1)}, u32[]{:S(2)}, u32[]{:S(2)}) async-start(f32[4,256,512]{2,0,1:T(4,128)} %copy.108), calls=%async_computation.2 | async-start | bytes 4194304 | tf_op jit(solution)/shard_map/all_to_all | solution.py:79
  293.1 340.9 %all-gather.2.cloned.1.call-start = ((), (), s32[]{:S(2)}) async-start(), calls=%async_computation.6 | async-start | bytes 2359296 | tf_op jit(solution)/shard_map/all_gather | solution.py:121
  341.9 2.7 collective-permute-start
  343.1 5.6 collective-permute-start.1
  366.4 1.4 collective-permute-start.2
  366.4 4.1 collective-permute-start.3
  377.8 24.7 %collective-permute-start.4 = (f32[16,1,258]{2,0,1:T(8,128)S(1)}, f32[16,1,258]{2,0,1:T(8,128)S(1)}, u32[]{:S(2)}, u32[]{:S(2)}) collective-permute-start(f32[16,1,258]{2,0,1:T(8,128)S(1)} %copy.118), channel_id=1, source_target_pairs={{1,0},{2,1},{3,2},{5,4},{6,5},{7,6},{9,8},{10,9},{11,10},{13,12},{... | collective-permute-start | bytes 49544 | tf_op jit(solution)/shard_map/ppermute | solution.py:19
  380.2 23.6 %collective-permute-start.5 = (f32[16,1,258]{2,0,1:T(8,128)S(1)}, f32[16,1,258]{2,0,1:T(8,128)S(1)}, u32[]{:S(2)}, u32[]{:S(2)}) collective-permute-start(f32[16,1,258]{2,0,1:T(8,128)S(1)} %copy.121), channel_id=1, source_target_pairs={{0,1},{1,2},{2,3},{4,5},{5,6},{6,7},{8,9},{9,10},{10,11},{12,13},{... | collective-permute-start | bytes 49544 | tf_op jit(solution)/shard_map/ppermute | solution.py:18
  438.1 5.3 collective-permute-start.6
  438.2 5.3 collective-permute-start.7
  464.1 11.1 %collective-permute-start.8 = (f32[4,16,1,258]{3,1,2,0:T(8,128)S(1)}, f32[4,16,1,258]{3,1,2,0:T(8,128)S(1)}, u32[]{:S(2)}, u32[]{:S(2)}) collective-permute-start(f32[4,16,1,258]{3,1,2,0:T(8,128)S(1)} %copy.126), channel_id=1, source_target_pairs={{0,1},{1,2},{2,3},{4,5},{5,6},{6,7},{8,9},{9,10},{10,11},{12,13},{... | collective-permute-start | bytes 198152 | tf_op jit(solution)/shard_map/ppermute | solution.py:18
  473.8 7.9 %collective-permute-start.9 = (f32[4,16,1,258]{3,1,2,0:T(8,128)S(1)}, f32[4,16,1,258]{3,1,2,0:T(8,128)S(1)}, u32[]{:S(2)}, u32[]{:S(2)}) collective-permute-start(f32[4,16,1,258]{3,1,2,0:T(8,128)S(1)} %copy.127), channel_id=1, source_target_pairs={{1,0},{2,1},{3,2},{5,4},{6,5},{7,6},{9,8},{10,9},{11,10},{13,12},{... | collective-permute-start | bytes 198152 | tf_op jit(solution)/shard_map/ppermute | solution.py:19
  513.8 17.6 %copy-start.1 = (f32[16,256,256]{1,0,2:T(8,128)S(1)}, f32[16,256,256]{1,0,2:T(8,128)}, u32[]{:S(2)}) copy-start(f32[16,256,256]{1,0,2:T(8,128)} %fusion.3) | copy-start | bytes 12582916
  554.8 3.1 collective-permute-start.10
  557.0 17.4 %collective-permute-start.11 = (f32[16,68,2]{1,0,2:T(8,128)S(1)}, f32[16,68,2]{1,0,2:T(8,128)S(1)}, u32[]{:S(2)}, u32[]{:S(2)}) collective-permute-start(f32[16,68,2]{1,0,2:T(8,128)S(1)} %copy.149), channel_id=1, source_target_pairs={{0,4},{4,8},{8,12},{12,16},{16,20},{20,24},{24,28},{28,0},{1,5},{5... | collective-permute-start | bytes 26120 | tf_op jit(solution)/shard_map/ppermute | solution.py:26
  581.8 6.5 collective-permute-start.12
  583.2 6.6 collective-permute-start.13
  636.2 9.2 %copy-start.5 = (f32[256,256]{1,0:T(8,128)S(1)}, f32[256,256]{1,0:T(8,128)}, u32[]{:S(2)}) copy-start(f32[256,256]{1,0:T(8,128)} %param.18) | copy-start | bytes 786436
  (2 other events, 7.8 us)
Sparse Core Ops, SparseCore 0:
  224.5 60.9 all-reduce.33
  607.0 27.0 all-gather.1
